TPU v7x, 32 devices: a whole 2x2x4 slice. The times are simulated.
32 devices in a mesh: group: 4 (over y, core), expert: 8 (over z, x).
Axes of the slice: x: 2, y: 2, z: 4, core: 2. Of those that a mesh axis runs over, the one named last changes fastest.
Arguments:
- tokens: bfloat16 [4096, 4096], P(('group', 'expert')), may hold values from -8 to 8
- router_weight: bfloat16 [4096, 128], replicated, may hold values from -4 to 4
- expert_dest: int32 [4096, 8], P(('group', 'expert')), may hold values from 0 to 127, all different within a row; in each aligned block of 128 rows (0 to 127, 128 to 255, ...) at most 9 rows name the same one
- group_capacity: int32 [4], replicated, may hold values from 4096 to 16383
- expert_capacity: int32 [128], replicated, may hold values from 128 to 511
- w_gate: bfloat16 [128, 4096, 768], P(('group', 'expert')), may hold values from -0.09375 to 0.09375
- w_up: bfloat16 [128, 4096, 768], P(('group', 'expert')), may hold values from -0.09375 to 0.09375
- w_down: bfloat16 [128, 768, 4096], P(('group', 'expert')), may hold values from -0.21875 to 0.21875
Outputs:
- mixed: bfloat16 [4096, 4096], P(('group', 'expert'))
- gating: float32 [4096, 8], P(('group', 'expert'))
Inputs may be any that keep to these rules, and one draw needn't show every extreme that they name: `expert_dest`: each token names 8 different experts; among the tokens of one device no expert is named more than 9 times, and that bound is reached.
All inputs are finite; a program needn't handle non-finite values.
Results may differ from a plain program's by a relative error of at most 0.0058.
Values may be sent and summed in bfloat16 or wider, within the bound.
No kernel may reach another device: no remote copies, remote signals or barrier semaphores. Data moves between devices by JAX's collectives and lax.ppermute only.
A program may use at most 256 MiB of HBM per device.

v0:
```python
import jax
import jax.numpy as jnp
from jax import lax
from jax.sharding import PartitionSpec as P

ITER1 = 10
ITER2 = 10
SLOT_CAP = 9


def balance(scores, gtarget, etarget, n_group, group_total, expert_total):
    rows, experts = scores.shape
    blocks = scores.reshape(rows, n_group, experts // n_group)
    kernel = jnp.sum(blocks, 2)

    def first(step, carry):
        scale_rows, scale_cols = carry
        scale_rows = 1.0 / jnp.sum(kernel * scale_cols[None, :], 1)
        scale_cols = gtarget / group_total(jnp.sum(kernel * scale_rows[:, None], 0))
        return (scale_rows, scale_cols)

    scale_rows, scale_cols = lax.fori_loop(
        0, ITER1, first, (jnp.ones((rows,), jnp.float32), jnp.ones((n_group,), jnp.float32))
    )
    plan = scale_rows[:, None] * kernel * scale_cols[None, :]

    def second(step, carry):
        row_fac, col_fac = carry
        row_fac = plan / jnp.sum(blocks * col_fac[None], 2)
        col_fac = etarget / expert_total(jnp.sum(blocks * row_fac[:, :, None], 0))
        return (row_fac, col_fac)

    row_fac, col_fac = lax.fori_loop(
        0,
        ITER2,
        second,
        (
            jnp.ones((rows, n_group), jnp.float32),
            jnp.ones((n_group, experts // n_group), jnp.float32),
        ),
    )
    return (row_fac[:, :, None] * blocks * col_fac[None]).reshape(rows, experts)


def per_device(
    tokens, router_weight, expert_dest, group_capacity, expert_capacity, w_gate, w_up, w_down
):
    tok_dev, width = tokens.shape
    experts = router_weight.shape[1]
    topk = expert_dest.shape[1]
    n_group = lax.axis_size("group")
    n_lane = lax.axis_size("expert")
    devices = n_group * n_lane
    exp_dev = w_gate.shape[0]
    logits = jnp.dot(tokens, router_weight, preferred_element_type=jnp.float32)
    scores = jnp.exp(logits)
    gcap = group_capacity.astype(jnp.float32)
    gtarget = tok_dev * devices * gcap / jnp.sum(gcap)
    ecap = expert_capacity.astype(jnp.float32).reshape(n_group, experts // n_group)
    etarget = (gtarget / jnp.sum(ecap, 1))[:, None] * ecap
    balanced = balance(
        scores,
        gtarget,
        etarget,
        n_group,
        lambda part: lax.psum(part, ("group", "expert")),
        lambda part: lax.psum(part, ("group", "expert")),
    )
    gating = jnp.take_along_axis(balanced, expert_dest, axis=1) * (experts / topk)
    flat_dest = expert_dest.reshape(-1)
    onehot = (flat_dest[:, None] == jnp.arange(experts, dtype=jnp.int32)[None, :]).astype(jnp.int32)
    position = jnp.sum(jnp.cumsum(onehot, 0) * onehot, 1) - 1
    slot = flat_dest * SLOT_CAP + position
    token_of = jnp.arange(tok_dev * topk, dtype=jnp.int32) // topk
    outgoing = jnp.zeros((experts * SLOT_CAP, width), jnp.bfloat16).at[slot].set(tokens[token_of])
    outgoing = outgoing.reshape(devices, exp_dev, SLOT_CAP, width)
    arrived = lax.all_to_all(outgoing, ("group", "expert"), split_axis=0, concat_axis=0, tiled=True)
    gate = jnp.einsum("skcd,kdf->skcf", arrived, w_gate, preferred_element_type=jnp.float32)
    up = jnp.einsum("skcd,kdf->skcf", arrived, w_up, preferred_element_type=jnp.float32)
    hidden = (jax.nn.silu(gate) * up).astype(jnp.bfloat16)
    returned = lax.all_to_all(
        jnp.einsum("skcf,kfd->skcd", hidden, w_down, preferred_element_type=jnp.float32).astype(
            jnp.bfloat16
        ),
        ("group", "expert"),
        split_axis=0,
        concat_axis=0,
        tiled=True,
    )
    expert_rows = returned.reshape(experts * SLOT_CAP, width)[slot]
    weighted = gating.reshape(-1, 1) * expert_rows.astype(jnp.float32)
    mixed = jnp.sum(weighted.reshape(tok_dev, topk, width), 1).astype(jnp.bfloat16)
    return (mixed, gating)


def solution(mesh):
    return jax.shard_map(
        per_device,
        mesh=mesh,
        in_specs=(
            P(("group", "expert"), None),
            P(),
            P(("group", "expert"), None),
            P(),
            P(),
            P(("group", "expert"), None, None),
            P(("group", "expert"), None, None),
            P(("group", "expert"), None, None),
        ),
        out_specs=(P(("group", "expert"), None), P(("group", "expert"), None)),
        check_vma=False,
    )
```

profile of v0, /device:TPU:0, one launch (start us, length us, event | category | flops | bytes accessed | tf_op | source)
XLA Modules:
  0.0 1429.2 jit_solution(244274422835837965)
XLA Ops:
  0.6 0.8 broadcast_multiply_fusion
  1.4 0.8 copy.73
  3.1 0.4 fusion.21
  3.5 7.7 gather_fusion
  11.3 18.4 %scatter_custom_fusion = bf16[1152,4096]{1,0:T(8,128)(2,1)} fusion(s32[1024]{0:T(1024)S(1)} %bitcast.66, bf16[1024,4096]{1,0:T(8,128)(2,1)} %gather_fusion, bf16[]{:T(256)} %constant.68.clone.1), kind=kCustom, calls=%fused_computation.22 | custom fusion | bytes 9437696 | tf_op jit(solution)/shard_map/scatter | solution.py:75
  29.7 15.1 %reshape.161 = bf16[32,4,9,4096]{3,2,1,0:T(8,128)(2,1)} reshape(bf16[1152,4096]{1,0:T(8,128)(2,1)} %scatter_custom_fusion) | data formatting | bytes 18874368 | tf_op jit(solution)/shard_map/reshape | solution.py:76
  44.8 12.6 copy.77
  57.3 214.5 %all_to_all.10 = bf16[32,4,9,4096]{3,1,2,0:T(4,128)(2,1)} all-to-all(bf16[32,4,9,4096]{3,1,2,0:T(4,128)(2,1)S(1)} %copy.77), channel_id=1, replica_groups=mesh['group'=4,'expert'=8] {'group','expert'}, dimensions={0} | all-to-all | bytes 18874368 | tf_op jit(solution)/shard_map/all_to_all | solution.py:77
  271.8 28.7 %fusion.2 = f32[4,32,9,768]{3,1,2,0:T(8,128)} fusion(bf16[4,4096,768]{2,1,0:T(8,128)(2,1)} %param.18, bf16[32,4,9,4096]{3,1,2,0:T(4,128)(2,1)} %all_to_all.10), kind=kOutput, calls=%fused_computation.13 | convolution fusion | flops 7247757312 | bytes 38141952 | tf_op jit(solution)/shard_map/skcd,kdf->skcf/dot_general | solution.py:79
  300.6 29.6 %fusion.13 = bf16[32,4,9,768]{3,0,2,1:T(8,128)(2,1)} fusion(f32[4,32,9,768]{3,1,2,0:T(8,128)} %fusion.2, bf16[4,4096,768]{2,1,0:T(8,128)(2,1)} %param.17, bf16[32,4,9,4096]{3,1,2,0:T(4,128)(2,1)} %all_to_all.10), kind=kOutput, calls=%fused_computation.25 | convolution fusion | flops 7253065728 | bytes 39911424 | tf_op jit(solution)/shard_map/skcd,kdf->skcf/dot_general | solution.py:78
  330.1 15.4 %convert_bitcast_fusion = bf16[32,4,9,4096]{3,0,2,1:T(8,128)(2,1)} fusion(bf16[32,4,9,768]{3,0,2,1:T(8,128)(2,1)} %fusion.13, bf16[4,768,4096]{2,1,0:T(8,128)(2,1)} %param.19), kind=kOutput, calls=%fused_computation.19 | convolution fusion | flops 7252475904 | bytes 36372480 | tf_op jit(solution)/shard_map/skcf,kfd->skcd/dot_general | solution.py:82
  345.5 13.4 copy.80
  358.9 3.8 all-to-all-start.1
  362.8 0.5 bitcast_reduce_fusion
  363.8 0.7 convert_reduce_fusion
  364.4 0.6 multiply_divide_fusion
  365.1 589.8 %while.26 = (s32[]{:T(128)}, f32[128]{0:T(128)}, f32[4]{0:T(128)S(1)}, f32[128,4]{0,1:T(4,128)S(1)}, f32[4]{0:T(128)S(1)}, /*index=5*/s32[]{:T(128)}, s32[]{:T(128)}) while((s32[]{:T(128)}, f32[128]{0:T(128)}, f32[4]{0:T(128)S(1)}, f32[128,4]{0,1:T(4,128)S(1)}, f32[4]{0:T(128)S(1)}, /*index=5*/s32[]{:T(128)}, s32[]{:T(128)}) %tuple.55), condition=%wide.region_6.7_spmd.clone, body=%wide.region_2.6_spmd.clone.sunk | while | flops 2059 | bytes 8459 | solution.py:22
  365.3 229.2 %psum.18 = f32[4]{0:T(128)S(1)} all-reduce(f32[4]{0:T(128)S(1)} %multiply_reduce_fusion.9), channel_id=1, replica_groups=mesh['group'=4,'expert'=8] {'group','expert'}, use_global_device_ids=true, to_apply=%region_5.0 | all-reduce | flops 4 | bytes 32 | tf_op jit(solution)/shard_map/while/body/eval_jaxpr/psum | solution.py:66
  594.8 38.4 %psum.18 = f32[4]{0:T(128)S(1)} all-reduce(f32[4]{0:T(128)S(1)} %multiply_reduce_fusion.9), channel_id=1, replica_groups=mesh['group'=4,'expert'=8] {'group','expert'}, use_global_device_ids=true, to_apply=%region_5.0 | all-reduce | flops 4 | bytes 32 | tf_op jit(solution)/shard_map/while/body/eval_jaxpr/psum | solution.py:66
  633.4 41.5 %psum.18 = f32[4]{0:T(128)S(1)} all-reduce(f32[4]{0:T(128)S(1)} %multiply_reduce_fusion.9), channel_id=1, replica_groups=mesh['group'=4,'expert'=8] {'group','expert'}, use_global_device_ids=true, to_apply=%region_5.0 | all-reduce | flops 4 | bytes 32 | tf_op jit(solution)/shard_map/while/body/eval_jaxpr/psum | solution.py:66
  675.2 38.4 %psum.18 = f32[4]{0:T(128)S(1)} all-reduce(f32[4]{0:T(128)S(1)} %multiply_reduce_fusion.9), channel_id=1, replica_groups=mesh['group'=4,'expert'=8] {'group','expert'}, use_global_device_ids=true, to_apply=%region_5.0 | all-reduce | flops 4 | bytes 32 | tf_op jit(solution)/shard_map/while/body/eval_jaxpr/psum | solution.py:66
  713.8 41.5 %psum.18 = f32[4]{0:T(128)S(1)} all-reduce(f32[4]{0:T(128)S(1)} %multiply_reduce_fusion.9), channel_id=1, replica_groups=mesh['group'=4,'expert'=8] {'group','expert'}, use_global_device_ids=true, to_apply=%region_5.0 | all-reduce | flops 4 | bytes 32 | tf_op jit(solution)/shard_map/while/body/eval_jaxpr/psum | solution.py:66
  755.6 38.4 %psum.18 = f32[4]{0:T(128)S(1)} all-reduce(f32[4]{0:T(128)S(1)} %multiply_reduce_fusion.9), channel_id=1, replica_groups=mesh['group'=4,'expert'=8] {'group','expert'}, use_global_device_ids=true, to_apply=%region_5.0 | all-reduce | flops 4 | bytes 32 | tf_op jit(solution)/shard_map/while/body/eval_jaxpr/psum | solution.py:66
  794.2 41.5 %psum.18 = f32[4]{0:T(128)S(1)} all-reduce(f32[4]{0:T(128)S(1)} %multiply_reduce_fusion.9), channel_id=1, replica_groups=mesh['group'=4,'expert'=8] {'group','expert'}, use_global_device_ids=true, to_apply=%region_5.0 | all-reduce | flops 4 | bytes 32 | tf_op jit(solution)/shard_map/while/body/eval_jaxpr/psum | solution.py:66
  835.9 38.5 %psum.18 = f32[4]{0:T(128)S(1)} all-reduce(f32[4]{0:T(128)S(1)} %multiply_reduce_fusion.9), channel_id=1, replica_groups=mesh['group'=4,'expert'=8] {'group','expert'}, use_global_device_ids=true, to_apply=%region_5.0 | all-reduce | flops 4 | bytes 32 | tf_op jit(solution)/shard_map/while/body/eval_jaxpr/psum | solution.py:66
  874.7 41.4 %psum.18 = f32[4]{0:T(128)S(1)} all-reduce(f32[4]{0:T(128)S(1)} %multiply_reduce_fusion.9), channel_id=1, replica_groups=mesh['group'=4,'expert'=8] {'group','expert'}, use_global_device_ids=true, to_apply=%region_5.0 | all-reduce | flops 4 | bytes 32 | tf_op jit(solution)/shard_map/while/body/eval_jaxpr/psum | solution.py:66
  916.3 38.6 %psum.18 = f32[4]{0:T(128)S(1)} all-reduce(f32[4]{0:T(128)S(1)} %multiply_reduce_fusion.9), channel_id=1, replica_groups=mesh['group'=4,'expert'=8] {'group','expert'}, use_global_device_ids=true, to_apply=%region_5.0 | all-reduce | flops 4 | bytes 32 | tf_op jit(solution)/shard_map/while/body/eval_jaxpr/psum | solution.py:66
  954.9 0.7 multiply_multiply_fusion
  955.9 405.0 %while.27 = (s32[]{:T(128)}, f32[128,4]{1,0:T(8,128)}, f32[4,32]{1,0:T(4,128)S(1)}, f32[128,4,32]{2,1,0:T(4,128)S(1)}, f32[128,4]{1,0:T(8,128)S(1)}, /*index=5*/f32[4,32]{1,0:T(4,128)S(1)}, s32[]{:T(128)}, s32[]{:T(128)}) while((s32[]{:T(128)}, f32[128,4]{1,0:T(8,128)}, f32[4,32]{1,0:T(4,128)S(1)}, f32[128,4,32]{2,1,0:T(4,128)S(1)}, ...), condition=%wide.region_12.0_spmd.clone, body=%wide.region_8.0_spmd.clone.sunk | while | flops 65795 | bytes 154243 | solution.py:33
  955.9 0.2 multiply_reduce_fusion.10
  956.3 41.3 %psum.19 = f32[4,32]{1,0:T(4,128)S(1)} all-reduce(f32[4,32]{1,0:T(4,128)S(1)} %multiply_reduce_fusion.11), channel_id=1, replica_groups=mesh['group'=4,'expert'=8] {'group','expert'}, use_global_device_ids=true, to_apply=%region_11.0 | all-reduce | flops 128 | bytes 1024 | tf_op jit(solution)/shard_map/while/body/eval_jaxpr/psum | solution.py:67
  997.7 0.2 multiply_reduce_fusion.10
  998.1 38.7 %psum.19 = f32[4,32]{1,0:T(4,128)S(1)} all-reduce(f32[4,32]{1,0:T(4,128)S(1)} %multiply_reduce_fusion.11), channel_id=1, replica_groups=mesh['group'=4,'expert'=8] {'group','expert'}, use_global_device_ids=true, to_apply=%region_11.0 | all-reduce | flops 128 | bytes 1024 | tf_op jit(solution)/shard_map/while/body/eval_jaxpr/psum | solution.py:67
  1036.9 0.2 multiply_reduce_fusion.10
  1037.3 41.2 %psum.19 = f32[4,32]{1,0:T(4,128)S(1)} all-reduce(f32[4,32]{1,0:T(4,128)S(1)} %multiply_reduce_fusion.11), channel_id=1, replica_groups=mesh['group'=4,'expert'=8] {'group','expert'}, use_global_device_ids=true, to_apply=%region_11.0 | all-reduce | flops 128 | bytes 1024 | tf_op jit(solution)/shard_map/while/body/eval_jaxpr/psum | solution.py:67
  1079.0 38.8 %psum.19 = f32[4,32]{1,0:T(4,128)S(1)} all-reduce(f32[4,32]{1,0:T(4,128)S(1)} %multiply_reduce_fusion.11), channel_id=1, replica_groups=mesh['group'=4,'expert'=8] {'group','expert'}, use_global_device_ids=true, to_apply=%region_11.0 | all-reduce | flops 128 | bytes 1024 | tf_op jit(solution)/shard_map/while/body/eval_jaxpr/psum | solution.py:67
  1118.3 41.2 %psum.19 = f32[4,32]{1,0:T(4,128)S(1)} all-reduce(f32[4,32]{1,0:T(4,128)S(1)} %multiply_reduce_fusion.11), channel_id=1, replica_groups=mesh['group'=4,'expert'=8] {'group','expert'}, use_global_device_ids=true, to_apply=%region_11.0 | all-reduce | flops 128 | bytes 1024 | tf_op jit(solution)/shard_map/while/body/eval_jaxpr/psum | solution.py:67
  1160.0 38.8 %psum.19 = f32[4,32]{1,0:T(4,128)S(1)} all-reduce(f32[4,32]{1,0:T(4,128)S(1)} %multiply_reduce_fusion.11), channel_id=1, replica_groups=mesh['group'=4,'expert'=8] {'group','expert'}, use_global_device_ids=true, to_apply=%region_11.0 | all-reduce | flops 128 | bytes 1024 | tf_op jit(solution)/shard_map/while/body/eval_jaxpr/psum | solution.py:67
  1199.3 41.2 %psum.19 = f32[4,32]{1,0:T(4,128)S(1)} all-reduce(f32[4,32]{1,0:T(4,128)S(1)} %multiply_reduce_fusion.11), channel_id=1, replica_groups=mesh['group'=4,'expert'=8] {'group','expert'}, use_global_device_ids=true, to_apply=%region_11.0 | all-reduce | flops 128 | bytes 1024 | tf_op jit(solution)/shard_map/while/body/eval_jaxpr/psum | solution.py:67
  1241.0 38.8 %psum.19 = f32[4,32]{1,0:T(4,128)S(1)} all-reduce(f32[4,32]{1,0:T(4,128)S(1)} %multiply_reduce_fusion.11), channel_id=1, replica_groups=mesh['group'=4,'expert'=8] {'group','expert'}, use_global_device_ids=true, to_apply=%region_11.0 | all-reduce | flops 128 | bytes 1024 | tf_op jit(solution)/shard_map/while/body/eval_jaxpr/psum | solution.py:67
  1280.3 41.2 %psum.19 = f32[4,32]{1,0:T(4,128)S(1)} all-reduce(f32[4,32]{1,0:T(4,128)S(1)} %multiply_reduce_fusion.11), channel_id=1, replica_groups=mesh['group'=4,'expert'=8] {'group','expert'}, use_global_device_ids=true, to_apply=%region_11.0 | all-reduce | flops 128 | bytes 1024 | tf_op jit(solution)/shard_map/while/body/eval_jaxpr/psum | solution.py:67
  1322.0 38.9 %psum.19 = f32[4,32]{1,0:T(4,128)S(1)} all-reduce(f32[4,32]{1,0:T(4,128)S(1)} %multiply_reduce_fusion.11), channel_id=1, replica_groups=mesh['group'=4,'expert'=8] {'group','expert'}, use_global_device_ids=true, to_apply=%region_11.0 | all-reduce | flops 128 | bytes 1024 | tf_op jit(solution)/shard_map/while/body/eval_jaxpr/psum | solution.py:67
  1360.9 0.9 copy.68
  1362.1 7.0 gather_fusion.2
  1369.4 10.7 copy.81
  1380.2 15.8 %reshape.162 = bf16[1152,4096]{1,0:T(8,128)(2,1)} reshape(bf16[32,4,9,4096]{3,2,1,0:T(8,128)(2,1)} %copy.81) | data formatting | bytes 18874368 | tf_op jit(solution)/shard_map/reshape | solution.py:90
  1396.0 20.1 %gather_fusion.1 = bf16[1024,4096]{1,0:T(8,128)(2,1)} fusion(bf16[1152,4096]{1,0:T(8,128)(2,1)} %reshape.162, s32[1024]{0:T(1024)S(1)} %broadcast_clamp_fusion), kind=kCustom, calls=%fused_computation.1 | custom fusion | bytes 16781312 | tf_op jit(solution)/shard_map/gather | solution.py:90
  1416.1 12.9 fusion.6
  (185 shorter events, 8.2 us)
Async XLA Ops:
  0.6 2.9 copy-start
  358.9 3.9 copy-start.2
  358.9 4.6 copy-start.7
  358.9 4.8 copy-start.6
  358.9 1002.9 %copy-start.3 = (s32[128,8]{0,1:T(8,128)S(1)}, s32[128,8]{0,1:T(8,128)}, u32[]{:S(2)}) copy-start(s32[128,8]{0,1:T(8,128)} %param.14) | copy-start | bytes 12292
  358.9 1010.5 %all-to-all-start.1 = ((bf16[32,4,9,4096]{3,1,2,0:T(4,128)(2,1)}), bf16[32,4,9,4096]{3,1,2,0:T(4,128)(2,1)}, u32[]{:S(2)}, u32[]{:S(2)}) async-start(bf16[32,4,9,4096]{3,1,2,0:T(4,128)(2,1)} %copy.80), calls=%async_computation.1 | async-start | bytes 18874368 | tf_op jit(solution)/shard_map/all_to_all | solution.py:81
  365.2 229.4 %copy-start.4 = (f32[128]{0:T(128)}, f32[128]{0:T(128)S(1)}, u32[]{:S(2)}) copy-start(f32[128]{0:T(128)S(1)} %broadcast_divide_fusion.2) | copy-start | bytes 1540 | tf_op jit(solution)/shard_map/while
  594.7 38.5 %copy-start.4 = (f32[128]{0:T(128)}, f32[128]{0:T(128)S(1)}, u32[]{:S(2)}) copy-start(f32[128]{0:T(128)S(1)} %broadcast_divide_fusion.2) | copy-start | bytes 1540 | tf_op jit(solution)/shard_map/while
  633.3 41.6 %copy-start.4 = (f32[128]{0:T(128)}, f32[128]{0:T(128)S(1)}, u32[]{:S(2)}) copy-start(f32[128]{0:T(128)S(1)} %broadcast_divide_fusion.2) | copy-start | bytes 1540 | tf_op jit(solution)/shard_map/while
  675.1 38.5 %copy-start.4 = (f32[128]{0:T(128)}, f32[128]{0:T(128)S(1)}, u32[]{:S(2)}) copy-start(f32[128]{0:T(128)S(1)} %broadcast_divide_fusion.2) | copy-start | bytes 1540 | tf_op jit(solution)/shard_map/while
  713.7 41.6 %copy-start.4 = (f32[128]{0:T(128)}, f32[128]{0:T(128)S(1)}, u32[]{:S(2)}) copy-start(f32[128]{0:T(128)S(1)} %broadcast_divide_fusion.2) | copy-start | bytes 1540 | tf_op jit(solution)/shard_map/while
  755.4 38.6 %copy-start.4 = (f32[128]{0:T(128)}, f32[128]{0:T(128)S(1)}, u32[]{:S(2)}) copy-start(f32[128]{0:T(128)S(1)} %broadcast_divide_fusion.2) | copy-start | bytes 1540 | tf_op jit(solution)/shard_map/while
  794.1 41.6 %copy-start.4 = (f32[128]{0:T(128)}, f32[128]{0:T(128)S(1)}, u32[]{:S(2)}) copy-start(f32[128]{0:T(128)S(1)} %broadcast_divide_fusion.2) | copy-start | bytes 1540 | tf_op jit(solution)/shard_map/while
  835.8 38.6 %copy-start.4 = (f32[128]{0:T(128)}, f32[128]{0:T(128)S(1)}, u32[]{:S(2)}) copy-start(f32[128]{0:T(128)S(1)} %broadcast_divide_fusion.2) | copy-start | bytes 1540 | tf_op jit(solution)/shard_map/while
  874.6 41.5 %copy-start.4 = (f32[128]{0:T(128)}, f32[128]{0:T(128)S(1)}, u32[]{:S(2)}) copy-start(f32[128]{0:T(128)S(1)} %broadcast_divide_fusion.2) | copy-start | bytes 1540 | tf_op jit(solution)/shard_map/while
  916.2 38.7 %copy-start.4 = (f32[128]{0:T(128)}, f32[128]{0:T(128)S(1)}, u32[]{:S(2)}) copy-start(f32[128]{0:T(128)S(1)} %broadcast_divide_fusion.2) | copy-start | bytes 1540 | tf_op jit(solution)/shard_map/while
  956.1 41.6 %copy-start.1 = (f32[128,4]{1,0:T(8,128)}, f32[128,4]{1,0:T(8,128)S(1)}, u32[]{:S(2)}) copy-start(f32[128,4]{1,0:T(8,128)S(1)} %div.73) | copy-start | bytes 6148 | tf_op jit(solution)/shard_map/while
  997.9 38.9 %copy-start.1 = (f32[128,4]{1,0:T(8,128)}, f32[128,4]{1,0:T(8,128)S(1)}, u32[]{:S(2)}) copy-start(f32[128,4]{1,0:T(8,128)S(1)} %div.73) | copy-start | bytes 6148 | tf_op jit(solution)/shard_map/while
  1037.1 41.5 %copy-start.1 = (f32[128,4]{1,0:T(8,128)}, f32[128,4]{1,0:T(8,128)S(1)}, u32[]{:S(2)}) copy-start(f32[128,4]{1,0:T(8,128)S(1)} %div.73) | copy-start | bytes 6148 | tf_op jit(solution)/shard_map/while
  1078.8 39.0 %copy-start.1 = (f32[128,4]{1,0:T(8,128)}, f32[128,4]{1,0:T(8,128)S(1)}, u32[]{:S(2)}) copy-start(f32[128,4]{1,0:T(8,128)S(1)} %div.73) | copy-start | bytes 6148 | tf_op jit(solution)/shard_map/while
  1118.1 41.4 %copy-start.1 = (f32[128,4]{1,0:T(8,128)}, f32[128,4]{1,0:T(8,128)S(1)}, u32[]{:S(2)}) copy-start(f32[128,4]{1,0:T(8,128)S(1)} %div.73) | copy-start | bytes 6148 | tf_op jit(solution)/shard_map/while
  1159.8 39.0 %copy-start.1 = (f32[128,4]{1,0:T(8,128)}, f32[128,4]{1,0:T(8,128)S(1)}, u32[]{:S(2)}) copy-start(f32[128,4]{1,0:T(8,128)S(1)} %div.73) | copy-start | bytes 6148 | tf_op jit(solution)/shard_map/while
  1199.1 41.4 %copy-start.1 = (f32[128,4]{1,0:T(8,128)}, f32[128,4]{1,0:T(8,128)S(1)}, u32[]{:S(2)}) copy-start(f32[128,4]{1,0:T(8,128)S(1)} %div.73) | copy-start | bytes 6148 | tf_op jit(solution)/shard_map/while
  1240.8 39.0 %copy-start.1 = (f32[128,4]{1,0:T(8,128)}, f32[128,4]{1,0:T(8,128)S(1)}, u32[]{:S(2)}) copy-start(f32[128,4]{1,0:T(8,128)S(1)} %div.73) | copy-start | bytes 6148 | tf_op jit(solution)/shard_map/while
  1280.0 41.4 %copy-start.1 = (f32[128,4]{1,0:T(8,128)}, f32[128,4]{1,0:T(8,128)S(1)}, u32[]{:S(2)}) copy-start(f32[128,4]{1,0:T(8,128)S(1)} %div.73) | copy-start | bytes 6148 | tf_op jit(solution)/shard_map/while
  1321.7 39.1 %copy-start.1 = (f32[128,4]{1,0:T(8,128)}, f32[128,4]{1,0:T(8,128)S(1)}, u32[]{:S(2)}) copy-start(f32[128,4]{1,0:T(8,128)S(1)} %div.73) | copy-start | bytes 6148 | tf_op jit(solution)/shard_map/while
  1369.3 10.9 copy-start.5
where the time goes:
time: 1440 us; the launch traced here: 1430 us
  blocking collectives  1200 us (83%)
  local copies, waits for them, and re-layouts  124 us (9%)
  matrix products  74.2 us (5%)
  other arithmetic  23.3 us (2%)
    psum x20, blocking collectives, per_device(): lax.psum(part, ('group', 'expert'))  987 us
    all_to_all x1, blocking collectives, per_device(): lax.all_to_all(outgoing, ('group', 'expert'), split_axis=0, concat_axis=0...  214 us
    dot_general x1, matrix products, per_device(): jnp.einsum('skcd,kdf->skcf', arrived, w_gate, preferred_element_type=jnp....  29.6 us
  transfers between devices with their start and end apart: 1, of which 0 were waited for; matrix products, arithmetic and copies ran while one was open for 1% of the time, Pallas kernels for 0%

commit v1 on v0

--- a/solution.py
+++ b/solution.py
@@ -64,7 +64,7 @@
         etarget,
         n_group,
         lambda part: lax.psum(part, ("group", "expert")),
-        lambda part: lax.psum(part, ("group", "expert")),
+        lambda part: lax.psum(lax.psum(part, "expert"), "group"),
     )
     gating = jnp.take_along_axis(balanced, expert_dest, axis=1) * (experts / topk)
     flat_dest = expert_dest.reshape(-1)

time: 1440 us -> 1280 us (0.89)
  blocking collectives: 1200 us -> 1040 us
    psum x20 -> x10, blocking collectives: 987 us -> 587 us  [per_device(): lax.psum(part, ('group', 'expert'))]
    psum x0 -> x20, blocking collectives: none -> 240 us  [the longest x10 183 us: per_device(): lax.psum(part, 'expert')]
where the time goes in v1:
time: 1280 us; the launch traced here: 1270 us
  blocking collectives  1040 us (81%)
  local copies, waits for them, and re-layouts  124 us (10%)
  matrix products  74.2 us (6%)
  other arithmetic  23.3 us (2%)
    psum x10, blocking collectives, per_device(): lax.psum(part, ('group', 'expert'))  587 us
    all_to_all x1, blocking collectives, per_device(): lax.all_to_all(outgoing, ('group', 'expert'), split_axis=0, concat_axis=0...  214 us
    psum x10, blocking collectives, per_device(): lax.psum(part, 'expert')  183 us
    psum x10, blocking collectives, per_device(): lax.psum(lax.psum(part, 'expert'), 'group')  56.9 us
    dot_general x1, matrix products, per_device(): jnp.einsum('skcd,kdf->skcf', arrived, w_gate, preferred_element_type=jnp....  29.6 us
    dot_general x1, matrix products, per_device(): jnp.einsum('skcd,kdf->skcf', arrived, w_up, preferred_element_type=jnp.fl...  28.7 us
    reshape x2, local copies, waits for them, and re-layouts, per_device(): outgoing = outgoing.reshape(devices, exp_dev, SLOT_CAP, width)  27.7 us
  transfers between devices with their start and end apart: 1, of which 0 were waited for; matrix products, arithmetic and copies ran while one was open for 1% of the time, Pallas kernels for 0%

profile of v1, /device:TPU:0, one launch (start us, length us, event | category | flops | bytes accessed | tf_op | source)
XLA Modules:
  0.0 1268.7 jit_solution(469630006628916467)
XLA Ops:
  3.5 7.7 gather_fusion
  11.3 18.4 %scatter_custom_fusion = bf16[1152,4096]{1,0:T(8,128)(2,1)} fusion(s32[1024]{0:T(1024)S(1)} %bitcast.66, bf16[1024,4096]{1,0:T(8,128)(2,1)} %gather_fusion, bf16[]{:T(256)} %constant.68.clone.1), kind=kCustom, calls=%fused_computation.22 | custom fusion | bytes 9437696 | tf_op jit(solution)/shard_map/scatter | solution.py:75
  29.7 15.1 %reshape.161 = bf16[32,4,9,4096]{3,2,1,0:T(8,128)(2,1)} reshape(bf16[1152,4096]{1,0:T(8,128)(2,1)} %scatter_custom_fusion) | data formatting | bytes 18874368 | tf_op jit(solution)/shard_map/reshape | solution.py:76
  44.8 12.6 copy.77
  57.3 214.5 %all_to_all.10 = bf16[32,4,9,4096]{3,1,2,0:T(4,128)(2,1)} all-to-all(bf16[32,4,9,4096]{3,1,2,0:T(4,128)(2,1)S(1)} %copy.77), channel_id=1, replica_groups=mesh['group'=4,'expert'=8] {'group','expert'}, dimensions={0} | all-to-all | bytes 18874368 | tf_op jit(solution)/shard_map/all_to_all | solution.py:77
  271.8 28.7 %fusion.2 = f32[4,32,9,768]{3,1,2,0:T(8,128)} fusion(bf16[4,4096,768]{2,1,0:T(8,128)(2,1)} %param.18, bf16[32,4,9,4096]{3,1,2,0:T(4,128)(2,1)} %all_to_all.10), kind=kOutput, calls=%fused_computation.13 | convolution fusion | flops 7247757312 | bytes 38141952 | tf_op jit(solution)/shard_map/skcd,kdf->skcf/dot_general | solution.py:79
  300.6 29.6 %fusion.13 = bf16[32,4,9,768]{3,0,2,1:T(8,128)(2,1)} fusion(f32[4,32,9,768]{3,1,2,0:T(8,128)} %fusion.2, bf16[4,4096,768]{2,1,0:T(8,128)(2,1)} %param.17, bf16[32,4,9,4096]{3,1,2,0:T(4,128)(2,1)} %all_to_all.10), kind=kOutput, calls=%fused_computation.25 | convolution fusion | flops 7253065728 | bytes 39911424 | tf_op jit(solution)/shard_map/skcd,kdf->skcf/dot_general | solution.py:78
  330.1 15.4 %convert_bitcast_fusion = bf16[32,4,9,4096]{3,0,2,1:T(8,128)(2,1)} fusion(bf16[32,4,9,768]{3,0,2,1:T(8,128)(2,1)} %fusion.13, bf16[4,768,4096]{2,1,0:T(8,128)(2,1)} %param.19), kind=kOutput, calls=%fused_computation.19 | convolution fusion | flops 7252475904 | bytes 36372480 | tf_op jit(solution)/shard_map/skcf,kfd->skcd/dot_general | solution.py:82
  345.5 13.4 %copy.80 = bf16[32,4,9,4096]{3,1,2,0:T(4,128)(2,1)} copy(bf16[32,4,9,4096]{3,0,2,1:T(8,128)(2,1)} %convert_bitcast_fusion) | data formatting | bytes 18874368 | tf_op jit(solution)/shard_map/convert_element_type | solution.py:82
  358.9 3.8 all-to-all-start.1
  365.1 589.8 %while.26 = (s32[]{:T(128)}, f32[128]{0:T(128)}, f32[4]{0:T(128)S(1)}, f32[128,4]{0,1:T(4,128)S(1)}, f32[4]{0:T(128)S(1)}, /*index=5*/s32[]{:T(128)}, s32[]{:T(128)}) while((s32[]{:T(128)}, f32[128]{0:T(128)}, f32[4]{0:T(128)S(1)}, f32[128,4]{0,1:T(4,128)S(1)}, f32[4]{0:T(128)S(1)}, /*index=5*/s32[]{:T(128)}, s32[]{:T(128)}) %tuple.55), condition=%wide.region_6.7_spmd.clone, body=%wide.region_2.6_spmd.clone.sunk | while | flops 2059 | bytes 8459 | solution.py:22
  365.3 229.2 %psum.27 = f32[4]{0:T(128)S(1)} all-reduce(f32[4]{0:T(128)S(1)} %multiply_reduce_fusion.9), channel_id=1, replica_groups=mesh['group'=4,'expert'=8] {'group','expert'}, use_global_device_ids=true, to_apply=%region_5.0 | all-reduce | flops 4 | bytes 32 | tf_op jit(solution)/shard_map/while/body/eval_jaxpr/psum | solution.py:66
  594.8 38.4 %psum.27 = f32[4]{0:T(128)S(1)} all-reduce(f32[4]{0:T(128)S(1)} %multiply_reduce_fusion.9), channel_id=1, replica_groups=mesh['group'=4,'expert'=8] {'group','expert'}, use_global_device_ids=true, to_apply=%region_5.0 | all-reduce | flops 4 | bytes 32 | tf_op jit(solution)/shard_map/while/body/eval_jaxpr/psum | solution.py:66
  633.4 41.5 %psum.27 = f32[4]{0:T(128)S(1)} all-reduce(f32[4]{0:T(128)S(1)} %multiply_reduce_fusion.9), channel_id=1, replica_groups=mesh['group'=4,'expert'=8] {'group','expert'}, use_global_device_ids=true, to_apply=%region_5.0 | all-reduce | flops 4 | bytes 32 | tf_op jit(solution)/shard_map/while/body/eval_jaxpr/psum | solution.py:66
  675.2 38.4 %psum.27 = f32[4]{0:T(128)S(1)} all-reduce(f32[4]{0:T(128)S(1)} %multiply_reduce_fusion.9), channel_id=1, replica_groups=mesh['group'=4,'expert'=8] {'group','expert'}, use_global_device_ids=true, to_apply=%region_5.0 | all-reduce | flops 4 | bytes 32 | tf_op jit(solution)/shard_map/while/body/eval_jaxpr/psum | solution.py:66
  713.8 41.5 %psum.27 = f32[4]{0:T(128)S(1)} all-reduce(f32[4]{0:T(128)S(1)} %multiply_reduce_fusion.9), channel_id=1, replica_groups=mesh['group'=4,'expert'=8] {'group','expert'}, use_global_device_ids=true, to_apply=%region_5.0 | all-reduce | flops 4 | bytes 32 | tf_op jit(solution)/shard_map/while/body/eval_jaxpr/psum | solution.py:66
  755.6 38.4 %psum.27 = f32[4]{0:T(128)S(1)} all-reduce(f32[4]{0:T(128)S(1)} %multiply_reduce_fusion.9), channel_id=1, replica_groups=mesh['group'=4,'expert'=8] {'group','expert'}, use_global_device_ids=true, to_apply=%region_5.0 | all-reduce | flops 4 | bytes 32 | tf_op jit(solution)/shard_map/while/body/eval_jaxpr/psum | solution.py:66
  794.2 41.5 %psum.27 = f32[4]{0:T(128)S(1)} all-reduce(f32[4]{0:T(128)S(1)} %multiply_reduce_fusion.9), channel_id=1, replica_groups=mesh['group'=4,'expert'=8] {'group','expert'}, use_global_device_ids=true, to_apply=%region_5.0 | all-reduce | flops 4 | bytes 32 | tf_op jit(solution)/shard_map/while/body/eval_jaxpr/psum | solution.py:66
  835.9 38.5 %psum.27 = f32[4]{0:T(128)S(1)} all-reduce(f32[4]{0:T(128)S(1)} %multiply_reduce_fusion.9), channel_id=1, replica_groups=mesh['group'=4,'expert'=8] {'group','expert'}, use_global_device_ids=true, to_apply=%region_5.0 | all-reduce | flops 4 | bytes 32 | tf_op jit(solution)/shard_map/while/body/eval_jaxpr/psum | solution.py:66
  874.7 41.4 %psum.27 = f32[4]{0:T(128)S(1)} all-reduce(f32[4]{0:T(128)S(1)} %multiply_reduce_fusion.9), channel_id=1, replica_groups=mesh['group'=4,'expert'=8] {'group','expert'}, use_global_device_ids=true, to_apply=%region_5.0 | all-reduce | flops 4 | bytes 32 | tf_op jit(solution)/shard_map/while/body/eval_jaxpr/psum | solution.py:66
  916.3 38.6 %psum.27 = f32[4]{0:T(128)S(1)} all-reduce(f32[4]{0:T(128)S(1)} %multiply_reduce_fusion.9), channel_id=1, replica_groups=mesh['group'=4,'expert'=8] {'group','expert'}, use_global_device_ids=true, to_apply=%region_5.0 | all-reduce | flops 4 | bytes 32 | tf_op jit(solution)/shard_map/while/body/eval_jaxpr/psum | solution.py:66
  955.9 244.5 %while.27 = (s32[]{:T(128)}, f32[128,4]{1,0:T(8,128)}, f32[4,32]{1,0:T(4,128)S(1)}, f32[128,4,32]{2,1,0:T(4,128)S(1)}, f32[128,4]{1,0:T(8,128)S(1)}, /*index=5*/f32[4,32]{1,0:T(4,128)S(1)}, s32[]{:T(128)}, s32[]{:T(128)}) while((s32[]{:T(128)}, f32[128,4]{1,0:T(8,128)}, f32[4,32]{1,0:T(4,128)S(1)}, f32[128,4,32]{2,1,0:T(4,128)S(1)}, ...), condition=%wide.region_13.0_spmd.clone, body=%wide.region_8.0_spmd.clone.sunk | while | flops 65923 | bytes 155267 | solution.py:33
  956.3 20.5 %psum.28 = f32[4,32]{1,0:T(4,128)S(1)} all-reduce(f32[4,32]{1,0:T(4,128)S(1)} %multiply_reduce_fusion.11), channel_id=1, replica_groups=mesh['group'=4,'expert'=8] {'expert'}, use_global_device_ids=true, to_apply=%region_11.0 | all-reduce | flops 128 | bytes 1024 | tf_op jit(solution)/shard_map/while/body/eval_jaxpr/psum | solution.py:67
  976.8 5.6 psum.29
  982.9 17.1 %psum.28 = f32[4,32]{1,0:T(4,128)S(1)} all-reduce(f32[4,32]{1,0:T(4,128)S(1)} %multiply_reduce_fusion.11), channel_id=1, replica_groups=mesh['group'=4,'expert'=8] {'expert'}, use_global_device_ids=true, to_apply=%region_11.0 | all-reduce | flops 128 | bytes 1024 | tf_op jit(solution)/shard_map/while/body/eval_jaxpr/psum | solution.py:67
  1000.1 5.6 psum.29
  1006.2 19.1 %psum.28 = f32[4,32]{1,0:T(4,128)S(1)} all-reduce(f32[4,32]{1,0:T(4,128)S(1)} %multiply_reduce_fusion.11), channel_id=1, replica_groups=mesh['group'=4,'expert'=8] {'expert'}, use_global_device_ids=true, to_apply=%region_11.0 | all-reduce | flops 128 | bytes 1024 | tf_op jit(solution)/shard_map/while/body/eval_jaxpr/psum | solution.py:67
  1025.3 5.6 psum.29
  1031.5 17.2 %psum.28 = f32[4,32]{1,0:T(4,128)S(1)} all-reduce(f32[4,32]{1,0:T(4,128)S(1)} %multiply_reduce_fusion.11), channel_id=1, replica_groups=mesh['group'=4,'expert'=8] {'expert'}, use_global_device_ids=true, to_apply=%region_11.0 | all-reduce | flops 128 | bytes 1024 | tf_op jit(solution)/shard_map/while/body/eval_jaxpr/psum | solution.py:67
  1048.6 5.6 psum.29
  1054.8 19.1 %psum.28 = f32[4,32]{1,0:T(4,128)S(1)} all-reduce(f32[4,32]{1,0:T(4,128)S(1)} %multiply_reduce_fusion.11), channel_id=1, replica_groups=mesh['group'=4,'expert'=8] {'expert'}, use_global_device_ids=true, to_apply=%region_11.0 | all-reduce | flops 128 | bytes 1024 | tf_op jit(solution)/shard_map/while/body/eval_jaxpr/psum | solution.py:67
  1073.9 5.6 psum.29
  1080.0 17.2 %psum.28 = f32[4,32]{1,0:T(4,128)S(1)} all-reduce(f32[4,32]{1,0:T(4,128)S(1)} %multiply_reduce_fusion.11), channel_id=1, replica_groups=mesh['group'=4,'expert'=8] {'expert'}, use_global_device_ids=true, to_apply=%region_11.0 | all-reduce | flops 128 | bytes 1024 | tf_op jit(solution)/shard_map/while/body/eval_jaxpr/psum | solution.py:67
  1097.2 5.7 psum.29
  1103.3 19.1 %psum.28 = f32[4,32]{1,0:T(4,128)S(1)} all-reduce(f32[4,32]{1,0:T(4,128)S(1)} %multiply_reduce_fusion.11), channel_id=1, replica_groups=mesh['group'=4,'expert'=8] {'expert'}, use_global_device_ids=true, to_apply=%region_11.0 | all-reduce | flops 128 | bytes 1024 | tf_op jit(solution)/shard_map/while/body/eval_jaxpr/psum | solution.py:67
  1122.5 5.8 psum.29
  1128.7 17.1 %psum.28 = f32[4,32]{1,0:T(4,128)S(1)} all-reduce(f32[4,32]{1,0:T(4,128)S(1)} %multiply_reduce_fusion.11), channel_id=1, replica_groups=mesh['group'=4,'expert'=8] {'expert'}, use_global_device_ids=true, to_apply=%region_11.0 | all-reduce | flops 128 | bytes 1024 | tf_op jit(solution)/shard_map/while/body/eval_jaxpr/psum | solution.py:67
  1145.9 5.8 psum.29
  1152.1 19.1 %psum.28 = f32[4,32]{1,0:T(4,128)S(1)} all-reduce(f32[4,32]{1,0:T(4,128)S(1)} %multiply_reduce_fusion.11), channel_id=1, replica_groups=mesh['group'=4,'expert'=8] {'expert'}, use_global_device_ids=true, to_apply=%region_11.0 | all-reduce | flops 128 | bytes 1024 | tf_op jit(solution)/shard_map/while/body/eval_jaxpr/psum | solution.py:67
  1171.2 5.8 psum.29
  1177.5 17.1 %psum.28 = f32[4,32]{1,0:T(4,128)S(1)} all-reduce(f32[4,32]{1,0:T(4,128)S(1)} %multiply_reduce_fusion.11), channel_id=1, replica_groups=mesh['group'=4,'expert'=8] {'expert'}, use_global_device_ids=true, to_apply=%region_11.0 | all-reduce | flops 128 | bytes 1024 | tf_op jit(solution)/shard_map/while/body/eval_jaxpr/psum | solution.py:67
  1194.6 5.8 psum.29
  1200.5 0.9 copy.68
  1201.7 7.0 gather_fusion.2
  1209.0 10.7 copy.81
  1219.7 15.8 %reshape.162 = bf16[1152,4096]{1,0:T(8,128)(2,1)} reshape(bf16[32,4,9,4096]{3,2,1,0:T(8,128)(2,1)} %copy.81) | data formatting | bytes 18874368 | tf_op jit(solution)/shard_map/reshape | solution.py:90
  1235.5 20.1 %gather_fusion.1 = bf16[1024,4096]{1,0:T(8,128)(2,1)} fusion(bf16[1152,4096]{1,0:T(8,128)(2,1)} %reshape.162, s32[1024]{0:T(1024)S(1)} %broadcast_clamp_fusion), kind=kCustom, calls=%fused_computation.1 | custom fusion | bytes 16781312 | tf_op jit(solution)/shard_map/gather | solution.py:90
  1255.7 12.9 %fusion.6 = bf16[128,4096]{1,0:T(8,128)(2,1)} fusion(bf16[1024,4096]{1,0:T(8,128)(2,1)} %gather_fusion.1, f32[128,8]{1,0:T(8,128)S(1)} %copy.71), kind=kLoop, calls=%fused_computation.18 | loop fusion | flops 12058624 | bytes 9441280 | tf_op jit(solution)/shard_map/reduce_sum | solution.py:92
  (195 shorter events, 13.4 us)
Async XLA Ops:
  0.6 2.9 copy-start
  358.9 3.9 copy-start.2
  358.9 4.6 copy-start.7
  358.9 4.8 copy-start.6
  358.9 842.5 %copy-start.3 = (s32[128,8]{0,1:T(8,128)S(1)}, s32[128,8]{0,1:T(8,128)}, u32[]{:S(2)}) copy-start(s32[128,8]{0,1:T(8,128)} %param.14) | copy-start | bytes 12292
  358.9 850.1 %all-to-all-start.1 = ((bf16[32,4,9,4096]{3,1,2,0:T(4,128)(2,1)}), bf16[32,4,9,4096]{3,1,2,0:T(4,128)(2,1)}, u32[]{:S(2)}, u32[]{:S(2)}) async-start(bf16[32,4,9,4096]{3,1,2,0:T(4,128)(2,1)} %copy.80), calls=%async_computation.1 | async-start | bytes 18874368 | tf_op jit(solution)/shard_map/all_to_all | solution.py:81
  365.2 229.4 %copy-start.4 = (f32[128]{0:T(128)}, f32[128]{0:T(128)S(1)}, u32[]{:S(2)}) copy-start(f32[128]{0:T(128)S(1)} %broadcast_divide_fusion.2) | copy-start | bytes 1540 | tf_op jit(solution)/shard_map/while
  594.7 38.5 %copy-start.4 = (f32[128]{0:T(128)}, f32[128]{0:T(128)S(1)}, u32[]{:S(2)}) copy-start(f32[128]{0:T(128)S(1)} %broadcast_divide_fusion.2) | copy-start | bytes 1540 | tf_op jit(solution)/shard_map/while
  633.3 41.6 %copy-start.4 = (f32[128]{0:T(128)}, f32[128]{0:T(128)S(1)}, u32[]{:S(2)}) copy-start(f32[128]{0:T(128)S(1)} %broadcast_divide_fusion.2) | copy-start | bytes 1540 | tf_op jit(solution)/shard_map/while
  675.1 38.5 %copy-start.4 = (f32[128]{0:T(128)}, f32[128]{0:T(128)S(1)}, u32[]{:S(2)}) copy-start(f32[128]{0:T(128)S(1)} %broadcast_divide_fusion.2) | copy-start | bytes 1540 | tf_op jit(solution)/shard_map/while
  713.7 41.6 %copy-start.4 = (f32[128]{0:T(128)}, f32[128]{0:T(128)S(1)}, u32[]{:S(2)}) copy-start(f32[128]{0:T(128)S(1)} %broadcast_divide_fusion.2) | copy-start | bytes 1540 | tf_op jit(solution)/shard_map/while
  755.4 38.6 %copy-start.4 = (f32[128]{0:T(128)}, f32[128]{0:T(128)S(1)}, u32[]{:S(2)}) copy-start(f32[128]{0:T(128)S(1)} %broadcast_divide_fusion.2) | copy-start | bytes 1540 | tf_op jit(solution)/shard_map/while
  794.1 41.6 %copy-start.4 = (f32[128]{0:T(128)}, f32[128]{0:T(128)S(1)}, u32[]{:S(2)}) copy-start(f32[128]{0:T(128)S(1)} %broadcast_divide_fusion.2) | copy-start | bytes 1540 | tf_op jit(solution)/shard_map/while
  835.8 38.6 %copy-start.4 = (f32[128]{0:T(128)}, f32[128]{0:T(128)S(1)}, u32[]{:S(2)}) copy-start(f32[128]{0:T(128)S(1)} %broadcast_divide_fusion.2) | copy-start | bytes 1540 | tf_op jit(solution)/shard_map/while
  874.6 41.5 %copy-start.4 = (f32[128]{0:T(128)}, f32[128]{0:T(128)S(1)}, u32[]{:S(2)}) copy-start(f32[128]{0:T(128)S(1)} %broadcast_divide_fusion.2) | copy-start | bytes 1540 | tf_op jit(solution)/shard_map/while
  916.2 38.7 %copy-start.4 = (f32[128]{0:T(128)}, f32[128]{0:T(128)S(1)}, u32[]{:S(2)}) copy-start(f32[128]{0:T(128)S(1)} %broadcast_divide_fusion.2) | copy-start | bytes 1540 | tf_op jit(solution)/shard_map/while
  956.1 26.3 %copy-start.1 = (f32[128,4]{1,0:T(8,128)}, f32[128,4]{1,0:T(8,128)S(1)}, u32[]{:S(2)}) copy-start(f32[128,4]{1,0:T(8,128)S(1)} %div.73) | copy-start | bytes 6148 | tf_op jit(solution)/shard_map/while
  982.7 23.0 %copy-start.1 = (f32[128,4]{1,0:T(8,128)}, f32[128,4]{1,0:T(8,128)S(1)}, u32[]{:S(2)}) copy-start(f32[128,4]{1,0:T(8,128)S(1)} %div.73) | copy-start | bytes 6148 | tf_op jit(solution)/shard_map/while
  1006.0 25.0 %copy-start.1 = (f32[128,4]{1,0:T(8,128)}, f32[128,4]{1,0:T(8,128)S(1)}, u32[]{:S(2)}) copy-start(f32[128,4]{1,0:T(8,128)S(1)} %div.73) | copy-start | bytes 6148 | tf_op jit(solution)/shard_map/while
  1031.3 23.0 %copy-start.1 = (f32[128,4]{1,0:T(8,128)}, f32[128,4]{1,0:T(8,128)S(1)}, u32[]{:S(2)}) copy-start(f32[128,4]{1,0:T(8,128)S(1)} %div.73) | copy-start | bytes 6148 | tf_op jit(solution)/shard_map/while
  1054.6 25.0 %copy-start.1 = (f32[128,4]{1,0:T(8,128)}, f32[128,4]{1,0:T(8,128)S(1)}, u32[]{:S(2)}) copy-start(f32[128,4]{1,0:T(8,128)S(1)} %div.73) | copy-start | bytes 6148 | tf_op jit(solution)/shard_map/while
  1079.8 23.1 %copy-start.1 = (f32[128,4]{1,0:T(8,128)}, f32[128,4]{1,0:T(8,128)S(1)}, u32[]{:S(2)}) copy-start(f32[128,4]{1,0:T(8,128)S(1)} %div.73) | copy-start | bytes 6148 | tf_op jit(solution)/shard_map/while
  1103.1 25.1 %copy-start.1 = (f32[128,4]{1,0:T(8,128)}, f32[128,4]{1,0:T(8,128)S(1)}, u32[]{:S(2)}) copy-start(f32[128,4]{1,0:T(8,128)S(1)} %div.73) | copy-start | bytes 6148 | tf_op jit(solution)/shard_map/while
  1128.5 23.1 %copy-start.1 = (f32[128,4]{1,0:T(8,128)}, f32[128,4]{1,0:T(8,128)S(1)}, u32[]{:S(2)}) copy-start(f32[128,4]{1,0:T(8,128)S(1)} %div.73) | copy-start | bytes 6148 | tf_op jit(solution)/shard_map/while
  1151.9 25.1 %copy-start.1 = (f32[128,4]{1,0:T(8,128)}, f32[128,4]{1,0:T(8,128)S(1)}, u32[]{:S(2)}) copy-start(f32[128,4]{1,0:T(8,128)S(1)} %div.73) | copy-start | bytes 6148 | tf_op jit(solution)/shard_map/while
  1177.3 23.1 %copy-start.1 = (f32[128,4]{1,0:T(8,128)}, f32[128,4]{1,0:T(8,128)S(1)}, u32[]{:S(2)}) copy-start(f32[128,4]{1,0:T(8,128)S(1)} %div.73) | copy-start | bytes 6148 | tf_op jit(solution)/shard_map/while
  1208.9 10.9 copy-start.5
